TPU v7x, 32 devices: a whole 2x2x4 slice. The times are simulated.
32 devices in a mesh: dp: 8 (over y, x, core), tensor: 4 (over z).
Axes of the slice: x: 2, y: 2, z: 4, core: 2. Of those that a mesh axis runs over, the one named last changes fastest.
Arguments:
- tokens: bfloat16 [12288, 2048], P(('dp', 'tensor')), may hold values from -6 to 6
- norm_attn: bfloat16 [2048], P('dp'), may hold values from 0.099609375 to 1.8984375
- w_query: bfloat16 [2048, 2048], P('dp', 'tensor'), may hold values from -0.125 to 0.125
- w_key: bfloat16 [2048, 128], P('dp'), may hold values from -0.125 to 0.125
- w_value: bfloat16 [2048, 128], P('dp'), may hold values from -0.125 to 0.125
- w_out: bfloat16 [2048, 2048], P('tensor', 'dp'), may hold values from -0.75 to 0.75
- norm_ffn: bfloat16 [2048], P('dp'), may hold values from 0.099609375 to 1.8984375
- w_gate: bfloat16 [2048, 5632], P('dp', 'tensor'), may hold values from -0.125 to 0.125
- w_up: bfloat16 [2048, 5632], P('dp', 'tensor'), may hold values from -0.125 to 0.125
- w_down: bfloat16 [5632, 2048], P('tensor', 'dp'), may hold values from -0.078125 to 0.078125
- segment_ids: int32 [12288], P('dp'), may hold values from 0 to 103, as said below
- parents: int32 [104], replicated, may hold values from 0 to 95, as said below
- positions: int32 [12288], P('dp'), may hold values from 0 to 927, as said below
- d_out: bfloat16 [12288, 2048], P(('dp', 'tensor')), may hold values from -6 to 6
- d_keys: bfloat16 [12288, 128], P(('dp', 'tensor')), may hold values from -6 to 6
- d_values: bfloat16 [12288, 128], P(('dp', 'tensor')), may hold values from -6 to 6
Outputs:
- out: bfloat16 [12288, 2048], P(('dp', 'tensor'))
- keys: bfloat16 [12288, 128], P('dp')
- values: bfloat16 [12288, 128], P('dp')
- d_x: float32 [12288, 2048], P(('dp', 'tensor'))
- g_norm_attn: float32 [2048], P('dp')
- g_query: float32 [2048, 2048], P('dp', 'tensor')
- g_key: float32 [2048, 128], P('dp')
- g_value: float32 [2048, 128], P('dp')
- g_out: float32 [2048, 2048], P('tensor', 'dp')
- g_norm_ffn: float32 [2048], P('dp')
- g_gate: float32 [2048, 5632], P('dp', 'tensor')
- g_up: float32 [2048, 5632], P('dp', 'tensor')
- g_down: float32 [5632, 2048], P('tensor', 'dp')
Inputs may be any that keep to these rules, and one draw needn't show every extreme that they name: `segment_ids`: tree t holds tokens t * 1536 to (t + 1) * 1536 - 1 and segments 13 t to 13 t + 12 in this order: a trunk of 768 tokens, four branches of 64 tokens, eight leaves whose two of each branch have lengths summing to 128, each leaf 64 // 2 tokens or more; ids never fall. `parents`: A trunk is its own parent, a branch's parent is its tree's trunk, a leaf's parent is a branch of its tree, and each branch is the parent of exactly two leaves. `positions`: counts up by one within a segment from 0 at a trunk's first token, from 768 at a branch's first token and from 832 at a leaf's first token.
All inputs are finite; a program needn't handle non-finite values.
Results may differ from a plain program's by a relative error of at most 0.022.
Values may be sent and summed in bfloat16 or wider, within the bound.
No kernel may reach another device: no remote copies, remote signals or barrier semaphores. Data moves between devices by JAX's collectives and lax.ppermute only.
A program may use at most 256 MiB of HBM per device.

v0:
```python
import jax
import jax.numpy as jnp
from jax import lax
from jax.sharding import PartitionSpec as P

HD = 128
QBLOCK = 512
norm_eps = 1e-05


def lookup(ids, table):
    hits = ids[:, None] == jnp.arange(table.shape[0], dtype=jnp.int32)[None, :]
    return jnp.sum(jnp.where(hits, table[None, :], 0), axis=1)


def path_mask(segment_block, first_block, second_block, place_block, segment, place):
    linked = (
        (segment[None, :] == segment_block[:, None])
        | (segment[None, :] == first_block[:, None])
        | (segment[None, :] == second_block[:, None])
    )
    return linked & (place[None, :] <= place_block[:, None])


def norm_back(value, scale, gain, grad):
    weighted = grad * gain
    return scale * weighted - value * (scale * scale * scale) * jnp.mean(
        weighted * value, axis=-1, keepdims=True
    )


def contract_rows(left, right):
    return lax.dot_general(
        left, right, (((0,), (0,)), ((), ())), preferred_element_type=jnp.float32
    )


def contract_cols(left, right):
    return lax.dot_general(
        left, right, (((1,), (1,)), ((), ())), preferred_element_type=jnp.float32
    )


def on_device(
    tokens,
    norm_attn,
    w_query,
    w_key,
    w_value,
    w_out,
    norm_ffn,
    w_gate,
    w_up,
    w_down,
    segment_ids,
    parents,
    positions,
    d_out,
    d_keys,
    d_values,
):
    score_scale = HD ** (-0.5)
    attn_gain, query_w, key_w, value_w, out_w = (
        lax.all_gather(norm_attn, "dp", axis=0, tiled=True),
        lax.all_gather(w_query, "dp", axis=0, tiled=True),
        lax.all_gather(w_key, "dp", axis=0, tiled=True),
        lax.all_gather(w_value, "dp", axis=0, tiled=True),
        lax.all_gather(w_out, "dp", axis=1, tiled=True),
    )
    ffn_gain, gate_w, up_w, down_w = (
        lax.all_gather(norm_ffn, "dp", axis=0, tiled=True),
        lax.all_gather(w_gate, "dp", axis=0, tiled=True),
        lax.all_gather(w_up, "dp", axis=0, tiled=True),
        lax.all_gather(w_down, "dp", axis=1, tiled=True),
    )
    attn_gain = attn_gain.astype(jnp.float32)
    ffn_gain = ffn_gain.astype(jnp.float32)
    residual = tokens.astype(jnp.float32)
    attn_scale = lax.rsqrt(jnp.mean(residual * residual, axis=-1, keepdims=True) + norm_eps)
    normed_own = (residual * attn_scale * attn_gain).astype(jnp.bfloat16)
    normed = lax.all_gather(normed_own, "tensor", axis=0, tiled=True)
    query = jnp.dot(normed, query_w, preferred_element_type=jnp.float32).astype(jnp.bfloat16)
    keys = jnp.dot(normed, key_w, preferred_element_type=jnp.float32).astype(jnp.bfloat16)
    values = jnp.dot(normed, value_w, preferred_element_type=jnp.float32).astype(jnp.bfloat16)
    total = normed.shape[0]
    blocks = total // QBLOCK
    heads = query.shape[1] // HD
    first_up = lookup(segment_ids, parents)
    second_up = lookup(first_up, parents)
    query_blocks = query.reshape(blocks, QBLOCK, heads, HD)
    id_blocks = (
        segment_ids.reshape(blocks, QBLOCK),
        first_up.reshape(blocks, QBLOCK),
        second_up.reshape(blocks, QBLOCK),
        positions.reshape(blocks, QBLOCK),
    )

    def attend(operand):
        query_block, segment_block, first_block, second_block, place_block = operand
        mask = path_mask(
            segment_block, first_block, second_block, place_block, segment_ids, positions
        )
        scores = (
            jnp.einsum("qhd,kd->hqk", query_block, keys, preferred_element_type=jnp.float32)
            * score_scale
        )
        scores = jnp.where(mask[None], scores, -1e30)
        peak = jnp.max(scores, axis=-1, keepdims=True)
        raised = jnp.exp(scores - peak)
        sums = jnp.sum(raised, axis=-1, keepdims=True)
        shares = (raised / sums).astype(jnp.bfloat16)
        mixed_block = jnp.einsum(
            "hqk,kd->qhd", shares, values, preferred_element_type=jnp.float32
        ).astype(jnp.bfloat16)
        return (mixed_block.reshape(QBLOCK, heads * HD), (peak + jnp.log(sums))[..., 0])

    mixed, log_totals = lax.map(attend, (query_blocks,) + id_blocks)
    mixed = mixed.reshape(total, heads * HD)
    attn_part = lax.psum_scatter(
        jnp.dot(mixed, out_w, preferred_element_type=jnp.float32),
        "tensor",
        scatter_dimension=0,
        tiled=True,
    )
    after_attn = residual + attn_part
    ffn_scale = lax.rsqrt(jnp.mean(after_attn * after_attn, axis=-1, keepdims=True) + norm_eps)
    ffn_own = (after_attn * ffn_scale * ffn_gain).astype(jnp.bfloat16)
    ffn_normed = lax.all_gather(ffn_own, "tensor", axis=0, tiled=True)
    gate = jnp.dot(ffn_normed, gate_w, preferred_element_type=jnp.float32)
    upward = jnp.dot(ffn_normed, up_w, preferred_element_type=jnp.float32)
    sigma = jax.nn.sigmoid(gate)
    hidden = (gate * sigma * upward).astype(jnp.bfloat16)
    ffn_part = lax.psum_scatter(
        jnp.dot(hidden, down_w, preferred_element_type=jnp.float32).astype(jnp.bfloat16),
        "tensor",
        scatter_dimension=0,
        tiled=True,
    ).astype(jnp.float32)
    output = (after_attn + ffn_part).astype(jnp.bfloat16)
    grad_full = lax.all_gather(d_out, "tensor", axis=0, tiled=True)
    down_grad = contract_rows(hidden, grad_full)
    hidden_grad = contract_cols(grad_full, down_w)
    gate_grad = (hidden_grad * upward * sigma * (1.0 + gate * (1.0 - sigma))).astype(jnp.bfloat16)
    up_grad = (hidden_grad * gate * sigma).astype(jnp.bfloat16)
    gate_w_grad = contract_rows(ffn_normed, gate_grad)
    up_w_grad = contract_rows(ffn_normed, up_grad)
    ffn_normed_grad = lax.psum_scatter(
        contract_cols(gate_grad, gate_w) + contract_cols(up_grad, up_w),
        "tensor",
        scatter_dimension=0,
        tiled=True,
    )
    after_grad = d_out.astype(jnp.float32) + norm_back(
        after_attn, ffn_scale, ffn_gain, ffn_normed_grad
    )
    ffn_gain_term = jnp.sum(ffn_normed_grad * after_attn * ffn_scale, axis=0)
    branch_full = lax.all_gather(after_grad.astype(jnp.bfloat16), "tensor", axis=0, tiled=True)
    out_w_grad = contract_rows(mixed, branch_full)
    mixed_grad = contract_cols(branch_full, out_w).astype(jnp.bfloat16)
    mixed_grad_blocks = mixed_grad.reshape(blocks, QBLOCK, heads, HD)

    def attend_back(carry, operand):
        key_acc, value_acc = carry
        (
            query_block,
            grad_block,
            log_block,
            segment_block,
            first_block,
            second_block,
            place_block,
        ) = operand
        mask = path_mask(
            segment_block, first_block, second_block, place_block, segment_ids, positions
        )
        scores = (
            jnp.einsum("qhd,kd->hqk", query_block, keys, preferred_element_type=jnp.float32)
            * score_scale
        )
        scores = jnp.where(mask[None], scores, -1e30)
        shares = jnp.exp(scores - log_block[:, :, None])
        low_shares = shares.astype(jnp.bfloat16)
        share_grad = jnp.einsum(
            "qhd,kd->hqk", grad_block, values, preferred_element_type=jnp.float32
        )
        value_acc = value_acc + jnp.einsum(
            "hqk,qhd->kd", low_shares, grad_block, preferred_element_type=jnp.float32
        )
        inner = jnp.sum(shares * share_grad, axis=-1, keepdims=True)
        score_grad = (shares * (share_grad - inner)).astype(jnp.bfloat16)
        query_grad_block = (
            score_scale
            * jnp.einsum("hqk,kd->qhd", score_grad, keys, preferred_element_type=jnp.float32)
        ).astype(jnp.bfloat16)
        key_acc = key_acc + score_scale * jnp.einsum(
            "hqk,qhd->kd", score_grad, query_block, preferred_element_type=jnp.float32
        )
        return ((key_acc, value_acc), query_grad_block.reshape(QBLOCK, heads * HD))

    empty = jnp.zeros((total, HD), jnp.float32)
    (key_acc, value_acc), query_grad = lax.scan(
        attend_back, (empty, empty), (query_blocks, mixed_grad_blocks, log_totals) + id_blocks
    )
    query_grad = query_grad.reshape(total, heads * HD)
    query_w_grad = contract_rows(normed, query_grad)
    normed_part = contract_cols(query_grad, query_w)
    normed_sum, key_sum, value_sum = (
        lax.psum_scatter(
            normed_part.astype(jnp.bfloat16), "tensor", scatter_dimension=0, tiled=True
        ).astype(jnp.float32),
        lax.psum_scatter(
            key_acc.astype(jnp.bfloat16), "tensor", scatter_dimension=0, tiled=True
        ).astype(jnp.float32),
        lax.psum_scatter(
            value_acc.astype(jnp.bfloat16), "tensor", scatter_dimension=0, tiled=True
        ).astype(jnp.float32),
    )
    key_grad = (key_sum + d_keys.astype(jnp.float32)).astype(jnp.bfloat16)
    value_grad = (value_sum + d_values.astype(jnp.float32)).astype(jnp.bfloat16)
    normed_grad = normed_sum + contract_cols(key_grad, key_w) + contract_cols(value_grad, value_w)
    key_w_term = contract_rows(normed_own, key_grad)
    value_w_term = contract_rows(normed_own, value_grad)
    input_grad = after_grad + norm_back(residual, attn_scale, attn_gain, normed_grad)
    attn_gain_term = jnp.sum(normed_grad * residual * attn_scale, axis=0)
    key_w_grad, value_w_grad, attn_gain_grad, ffn_gain_grad = (
        lax.psum(key_w_term.astype(jnp.bfloat16), "tensor").astype(jnp.float32),
        lax.psum(value_w_term.astype(jnp.bfloat16), "tensor").astype(jnp.float32),
        lax.psum(attn_gain_term.astype(jnp.bfloat16), "tensor").astype(jnp.float32),
        lax.psum(ffn_gain_term.astype(jnp.bfloat16), "tensor").astype(jnp.float32),
    )
    (
        attn_gain_part,
        query_part,
        key_part,
        value_part,
        out_part,
        ffn_gain_part,
        gate_part,
        up_part,
        down_part,
    ) = (
        lax.psum_scatter(
            attn_gain_grad.astype(jnp.bfloat16), "dp", scatter_dimension=0, tiled=True
        ).astype(jnp.float32),
        lax.psum_scatter(
            query_w_grad.astype(jnp.bfloat16), "dp", scatter_dimension=0, tiled=True
        ).astype(jnp.float32),
        lax.psum_scatter(
            key_w_grad.astype(jnp.bfloat16), "dp", scatter_dimension=0, tiled=True
        ).astype(jnp.float32),
        lax.psum_scatter(
            value_w_grad.astype(jnp.bfloat16), "dp", scatter_dimension=0, tiled=True
        ).astype(jnp.float32),
        lax.psum_scatter(
            out_w_grad.astype(jnp.bfloat16), "dp", scatter_dimension=1, tiled=True
        ).astype(jnp.float32),
        lax.psum_scatter(
            ffn_gain_grad.astype(jnp.bfloat16), "dp", scatter_dimension=0, tiled=True
        ).astype(jnp.float32),
        lax.psum_scatter(
            gate_w_grad.astype(jnp.bfloat16), "dp", scatter_dimension=0, tiled=True
        ).astype(jnp.float32),
        lax.psum_scatter(
            up_w_grad.astype(jnp.bfloat16), "dp", scatter_dimension=0, tiled=True
        ).astype(jnp.float32),
        lax.psum_scatter(
            down_grad.astype(jnp.bfloat16), "dp", scatter_dimension=1, tiled=True
        ).astype(jnp.float32),
    )
    return (
        output,
        keys,
        values,
        input_grad,
        attn_gain_part,
        query_part,
        key_part,
        value_part,
        out_part,
        ffn_gain_part,
        gate_part,
        up_part,
        down_part,
    )


def solution(mesh):
    in_specs = (
        P(("dp", "tensor"), None),
        P("dp"),
        P("dp", "tensor"),
        P("dp", None),
        P("dp", None),
        P("tensor", "dp"),
        P("dp"),
        P("dp", "tensor"),
        P("dp", "tensor"),
        P("tensor", "dp"),
        P("dp"),
        P(),
        P("dp"),
        P(("dp", "tensor"), None),
        P(("dp", "tensor"), None),
        P(("dp", "tensor"), None),
    )
    out_specs = (
        P(("dp", "tensor"), None),
        P("dp", None),
        P("dp", None),
        P(("dp", "tensor"), None),
        P("dp"),
        P("dp", "tensor"),
        P("dp", None),
        P("dp", None),
        P("tensor", "dp"),
        P("dp"),
        P("dp", "tensor"),
        P("dp", "tensor"),
        P("tensor", "dp"),
    )
    return jax.shard_map(
        on_device, mesh=mesh, in_specs=in_specs, out_specs=out_specs, check_vma=False
    )
```

profile of v0, /device:TPU:0, one launch (start us, length us, event | category | flops | bytes accessed | tf_op | source)
XLA Modules:
  0.0 1988.7 jit_solution(13247573112457298185)
XLA Ops:
  10.4 10.3 all-gather
  26.3 9.8 all_gather.42
  36.1 8.9 all_gather.43
  45.0 95.1 %all-gather.12.cloned.1.call-done = bf16[1536,2048]{1,0:T(8,128)(2,1)} async-done(((bf16[384,2048]{1,0:T(8,128)(2,1)}), bf16[1536,2048]{1,0:T(8,128)(2,1)}) %all-gather.12.cloned.1.call-update) | async-done | bytes 6291472 | tf_op jit(solution)/shard_map/all_gather | solution.py:81
  144.9 23.3 %all-gather.14.cloned.1.call-done = bf16[2048,512]{1,0:T(8,128)(2,1)} async-done(((bf16[256,512]{1,0:T(8,128)(2,1)}), bf16[2048,512]{1,0:T(8,128)(2,1)}) %all-gather.14.cloned.1.call-update) | async-done | bytes 2097168 | tf_op jit(solution)/shard_map/all_gather | solution.py:65
  168.2 8.0 convolution_convert_fusion.8
  184.9 40.4 %while.27 = (s32[]{:T(128)}, bf16[3,512,512]{2,1,0:T(8,128)(2,1)S(1)}, f32[3,4,512]{2,1,0:T(4,128)S(1)}, s32[1536]{0:T(1024)S(1)}, s32[3,512]{1,0:T(4,128)S(1)},...) while((s32[]{:T(128)}, ...), condition=%wide.region_6.7_spmd, body=%wide.region_3.6_spmd.sunk | while | flops 1654126592 | bytes 44929176 | solution.py:117
  225.4 8.6 fusion.48
  234.7 8.8 all-gather.1
  243.5 202.5 %reduce-scatter.14.cloned.1.call-done = f32[384,2048]{1,0:T(8,128)} async-done(((f32[1536,2048]{1,0:T(8,128)}), f32[384,2048]{1,0:T(8,128)}) %reduce-scatter.14.cloned.1.call-update) | async-done | bytes 3145744 | tf_op jit(solution)/shard_map/reduce_scatter | solution.py:119
  452.7 39.5 %all-gather.22.cloned.1.call-done = bf16[2048,1408]{1,0:T(8,128)(2,1)} async-done(((bf16[256,1408]{1,0:T(8,128)(2,1)}), bf16[2048,1408]{1,0:T(8,128)(2,1)}) %all-gather.22.cloned.1.call-update) | async-done | bytes 5767184 | tf_op jit(solution)/shard_map/all_gather | solution.py:73
  492.1 117.4 %all-gather.18.cloned.1.call-done = bf16[1536,2048]{1,0:T(8,128)(2,1)} async-done(((bf16[384,2048]{1,0:T(8,128)(2,1)}), bf16[1536,2048]{1,0:T(8,128)(2,1)}) %all-gather.18.cloned.1.call-update) | async-done | bytes 6291472 | tf_op jit(solution)/shard_map/all_gather | solution.py:128
  609.5 15.3 fusion.50
  624.8 28.2 %all-gather.20.cloned.1.call-done = bf16[2048,1408]{1,0:T(8,128)(2,1)} async-done(((bf16[256,1408]{1,0:T(8,128)(2,1)}), bf16[2048,1408]{1,0:T(8,128)(2,1)}) %all-gather.20.cloned.1.call-update) | async-done | bytes 5767184 | tf_op jit(solution)/shard_map/all_gather | solution.py:72
  653.0 15.1 fusion.49
  668.1 101.8 %all-gather.26.cloned.1.call-done = bf16[1536,2048]{1,0:T(8,128)(2,1)} async-done(((bf16[384,2048]{1,0:T(8,128)(2,1)}), bf16[1536,2048]{1,0:T(8,128)(2,1)}) %all-gather.26.cloned.1.call-update) | async-done | bytes 6291472 | tf_op jit(solution)/shard_map/all_gather | solution.py:140
  769.9 44.5 %all-gather.24.cloned.1.call-done = bf16[1408,2048]{1,0:T(8,128)(2,1)} async-done(((bf16[1408,256]{1,0:T(8,128)(2,1)}), bf16[1408,2048]{1,0:T(8,128)(2,1)}) %all-gather.24.cloned.1.call-update) | async-done | bytes 5767184 | tf_op jit(solution)/shard_map/all_gather | solution.py:74
  814.4 22.9 %multiply_convert_fusion = (bf16[1536,1408]{1,0:T(8,128)(2,1)}, bf16[1536,1408]{1,0:T(8,128)(2,1)}, bf16[1536,1408]{1,0:T(8,128)(2,1)}) fusion(f32[1536,1408]{1,0:T(8,128)} %fusion.49, f32[1536,1408]{1,0:T(8,128)} %fusion.50, bf16[1536,2048]{1,0:T(8,128)(2,1)} %all-gather.26.cloned.1.call-done, bf16[1408,2048]{1,0:T(8,128)(2,1)} %all-gather.24.cloned.1.call-done), kind=kOutput, calls=%fused_computation.58 | convolution fusion | flops 8892973056 | bytes 42336256 | tf_op jit(solution)/shard_map/dot_general | solution.py:39
  837.4 16.6 fusion.51
  854.0 16.4 convolution_add_fusion
  870.5 15.0 convolution_convert_fusion.4
  885.6 196.9 %reduce-scatter.18.cloned.1.call-done = f32[384,2048]{1,0:T(8,128)} async-done(((f32[1536,2048]{1,0:T(8,128)}), f32[384,2048]{1,0:T(8,128)}) %reduce-scatter.18.cloned.1.call-update) | async-done | bytes 3145744 | tf_op jit(solution)/shard_map/reduce_scatter | solution.py:147
  1085.7 110.9 %reduce-scatter.16.cloned.1.call-done = bf16[384,2048]{1,0:T(8,128)(2,1)} async-done(((bf16[1536,2048]{1,0:T(8,128)(2,1)}), bf16[384,2048]{1,0:T(8,128)(2,1)}) %reduce-scatter.16.cloned.1.call-update) | async-done | bytes 1572880 | tf_op jit(solution)/shard_map/reduce_scatter | solution.py:133
  1196.6 6.7 fusion.47
  1205.3 114.1 %all-gather.28.cloned.1.call-done = bf16[1536,2048]{1,0:T(8,128)(2,1)} async-done(((bf16[384,2048]{1,0:T(8,128)(2,1)}), bf16[1536,2048]{1,0:T(8,128)(2,1)}) %all-gather.28.cloned.1.call-update) | async-done | bytes 6291472 | tf_op jit(solution)/shard_map/all_gather | solution.py:157
  1319.4 6.9 convolution_convert_fusion.7
  1329.6 71.5 %while.28 = (s32[]{:T(128)}, f32[1536,128]{1,0:T(8,128)}, f32[1536,128]{1,0:T(8,128)S(1)}, bf16[3,512,512]{2,1,0:T(8,128)(2,1)}, s32[1536]{0:T(1024)S(1)}, /*ind...) while((s32[]{:T(128)}, f32[1536,128]{1,0:T(8,128)}, ...), condition=%wide.region_14.15_spmd.clone, body=%wide.region_12.14_spmd.clone.sunk | while | flops 4061853696 | bytes 139145552 | solution.py:201
  1334.9 5.6 fusion.117
  1358.8 5.6 fusion.117
  1382.6 5.6 fusion.117
  1404.3 17.9 reduce-scatter.22.cloned.1.call-done
  1425.1 18.7 reduce-scatter.24.cloned.1.call-done
  1446.2 14.3 convolution_convert_fusion
  1460.6 15.0 convolution_convert_fusion.1
  1475.9 15.0 convolution_convert_fusion.2
  1491.0 26.8 %reduce-scatter.38.cloned.1.call-done = bf16[256,128]{1,0:T(8,128)(2,1)} async-done(((bf16[2048,128]{1,0:T(8,128)(2,1)}), bf16[256,128]{1,0:T(8,128)(2,1)}) %reduce-scatter.38.cloned.1.call-update) | async-done | bytes 65552 | tf_op jit(solution)/shard_map/reduce_scatter | solution.py:251
  1517.9 7.8 convolution_convert_fusion.6
  1525.8 7.9 convolution_convert_fusion.5
  1534.0 7.2 convolution_convert_fusion.3
  1543.1 37.1 %reduce-scatter.34.cloned.1.call-done = bf16[1408,256]{1,0:T(8,128)(2,1)} async-done(((bf16[1408,2048]{1,0:T(8,128)(2,1)}), bf16[1408,256]{1,0:T(8,128)(2,1)}) %reduce-scatter.34.cloned.1.call-update) | async-done | bytes 720912 | tf_op jit(solution)/shard_map/reduce_scatter | solution.py:266
  1582.5 60.4 %reduce-scatter.32.cloned.1.call-done = bf16[256,1408]{1,0:T(8,128)(2,1)} async-done(((bf16[2048,1408]{1,0:T(8,128)(2,1)}), bf16[256,1408]{1,0:T(8,128)(2,1)}) %reduce-scatter.32.cloned.1.call-update) | async-done | bytes 720912 | tf_op jit(solution)/shard_map/reduce_scatter | solution.py:263
  1645.3 60.2 %reduce-scatter.30.cloned.1.call-done = bf16[256,1408]{1,0:T(8,128)(2,1)} async-done(((bf16[2048,1408]{1,0:T(8,128)(2,1)}), bf16[256,1408]{1,0:T(8,128)(2,1)}) %reduce-scatter.30.cloned.1.call-update) | async-done | bytes 720912 | tf_op jit(solution)/shard_map/reduce_scatter | solution.py:260
  1710.0 32.3 %all-reduce.7.cloned.1.call-done = (bf16[256,128]{1,0:T(8,128)(2,1)}, bf16[256,128]{1,0:T(8,128)(2,1)}) async-done(((bf16[256,128]{1,0:T(8,128)(2,1)}, bf16[256,128]{1,0:T(8,128)(2,1)}), (bf16[256,128]{1,0:T(8,128)(2,1)}, bf16[256,128]{1,0:T(8,128)(2,1)})) %all-reduce.7.cloned.1.call-update) | async-done | bytes 131088 | tf_op jit(solution)/shard_map/psum | solution.py:226
  1745.3 41.2 %reduce-scatter.26.cloned.1.call-done = bf16[256,512]{1,0:T(8,128)(2,1)} async-done(((bf16[2048,512]{1,0:T(8,128)(2,1)}), bf16[256,512]{1,0:T(8,128)(2,1)}) %reduce-scatter.26.cloned.1.call-update) | async-done | bytes 262160 | tf_op jit(solution)/shard_map/reduce_scatter | solution.py:245
  1788.4 43.1 %reduce-scatter.28.cloned.1.call-done = bf16[512,256]{1,0:T(8,128)(2,1)} async-done(((bf16[512,2048]{1,0:T(8,128)(2,1)}), bf16[512,256]{1,0:T(8,128)(2,1)}) %reduce-scatter.28.cloned.1.call-update) | async-done | bytes 262160 | tf_op jit(solution)/shard_map/reduce_scatter | solution.py:254
  1833.3 111.3 %reduce-scatter.20.cloned.1.call-done = bf16[384,2048]{1,0:T(8,128)(2,1)} async-done(((bf16[1536,2048]{1,0:T(8,128)(2,1)}), bf16[384,2048]{1,0:T(8,128)(2,1)}) %reduce-scatter.20.cloned.1.call-update) | async-done | bytes 1572880 | tf_op jit(solution)/shard_map/reduce_scatter | solution.py:208
  1949.9 14.0 all-reduce.2
  1964.0 11.1 all-reduce.3
  (243 shorter events, 171.1 us)
Async XLA Ops:
  7.2 18.7 copy-start.15
  7.2 18.7 copy-start.29
  7.2 19.1 copy-start.16
  7.2 19.1 copy-start.23
  7.2 28.9 %copy-start.24 = (bf16[256,128]{1,0:T(8,128)(2,1)S(1)}, bf16[256,128]{1,0:T(8,128)(2,1)}, u32[]{:S(2)}) copy-start(bf16[256,128]{1,0:T(8,128)(2,1)} %param.24) | copy-start | bytes 196612
  7.2 132.9 %all-gather.12.cloned.1.call-start = ((), (), s32[]{:S(2)}) async-start(), calls=%async_computation.13 | async-start | bytes 7864320 | tf_op jit(solution)/shard_map/all_gather | solution.py:81
  10.4 134.3 %copy-start.25 = (f32[384]{0:T(512)}, f32[384]{0:T(512)S(1)}, u32[]{:S(2)}) copy-start(f32[384]{0:T(512)S(1)} %get-tuple-element.401) | copy-start | bytes 4612
  24.3 143.9 %all-gather.14.cloned.1.call-start = ((), (), s32[]{:S(2)}) async-start(), calls=%async_computation.14 | async-start | bytes 2359296 | tf_op jit(solution)/shard_map/all_gather | solution.py:65
  25.1 200.3 %all-gather.16.cloned.1.call-start = ((), (), s32[]{:S(2)}) async-start(), calls=%async_computation.15 | async-start | bytes 2359296 | tf_op jit(solution)/shard_map/all_gather | solution.py:68
  25.8 420.2 %reduce-scatter.14.cloned.1.call-start = ((), (), s32[]{:S(2)}) async-start(), calls=%async_computation.16 | async-start | bytes 15728640 | tf_op jit(solution)/shard_map/reduce_scatter | solution.py:119
  36.1 144.1 %copy-start.10 = (bf16[2048,128]{1,0:T(8,128)(2,1)}, bf16[2048,128]{1,0:T(8,128)(2,1)S(1)}, u32[]{:S(2)}) copy-start(bf16[2048,128]{1,0:T(8,128)(2,1)S(1)} %all_gather.42) | copy-start | bytes 1572868
  45.0 123.2 %copy-start.8 = (bf16[2048,128]{1,0:T(8,128)(2,1)}, bf16[2048,128]{1,0:T(8,128)(2,1)S(1)}, u32[]{:S(2)}) copy-start(bf16[2048,128]{1,0:T(8,128)(2,1)S(1)} %all_gather.43) | copy-start | bytes 1572868
  144.7 31.4 %copy-start.5 = (bf16[1536,128]{1,0:T(8,128)(2,1)}, bf16[1536,128]{1,0:T(8,128)(2,1)S(1)}, u32[]{:S(2)}) copy-start(bf16[1536,128]{1,0:T(8,128)(2,1)S(1)} %convolution_convert_fusion.11) | copy-start | bytes 1179652
  225.4 8.6 copy-start.6
  225.4 8.6 copy-start.13
  234.0 258.1 %all-gather.22.cloned.1.call-start = ((), (), s32[]{:S(2)}) async-start(), calls=%async_computation.19 | async-start | bytes 6488064 | tf_op jit(solution)/shard_map/all_gather | solution.py:73
  234.6 374.9 %all-gather.18.cloned.1.call-start = ((), (), s32[]{:S(2)}) async-start(), calls=%async_computation.17 | async-start | bytes 7864320 | tf_op jit(solution)/shard_map/all_gather | solution.py:128
  450.4 202.6 %all-gather.20.cloned.1.call-start = ((), (), s32[]{:S(2)}) async-start(), calls=%async_computation.18 | async-start | bytes 6488064 | tf_op jit(solution)/shard_map/all_gather | solution.py:72
  451.1 318.8 %all-gather.26.cloned.1.call-start = ((), (), s32[]{:S(2)}) async-start(), calls=%async_computation.22 | async-start | bytes 7864320 | tf_op jit(solution)/shard_map/all_gather | solution.py:140
  451.9 362.6 %all-gather.24.cloned.1.call-start = ((), (), s32[]{:S(2)}) async-start(), calls=%async_computation.20 | async-start | bytes 6488064 | tf_op jit(solution)/shard_map/all_gather | solution.py:74
  452.6 629.9 %reduce-scatter.18.cloned.1.call-start = ((), (), s32[]{:S(2)}) async-start(), calls=%async_computation.23 | async-start | bytes 15728640 | tf_op jit(solution)/shard_map/reduce_scatter | solution.py:147
  837.4 16.6 copy-start.32
  870.5 326.1 %reduce-scatter.16.cloned.1.call-start = ((), (), s32[]{:S(2)}) async-start(), calls=%async_computation.21 | async-start | bytes 7864320 | tf_op jit(solution)/shard_map/reduce_scatter | solution.py:133
  885.6 433.8 %all-gather.28.cloned.1.call-start = ((), (), s32[]{:S(2)}) async-start(), calls=%async_computation.24 | async-start | bytes 7864320 | tf_op jit(solution)/shard_map/all_gather | solution.py:157
  1203.3 218.8 %reduce-scatter.22.cloned.1.call-start = ((), (), s32[]{:S(2)}) async-start(), calls=%async_computation.26 | async-start | bytes 491520 | tf_op jit(solution)/shard_map/reduce_scatter | solution.py:211
  1401.1 42.7 %copy-start.4 = (bf16[384,2048]{1,0:T(8,128)(2,1)S(1)}, bf16[384,2048]{1,0:T(8,128)(2,1)}, u32[]{:S(2)}) copy-start(bf16[384,2048]{1,0:T(8,128)(2,1)} %fusion.39) | copy-start | bytes 4718596
  1401.1 42.7 %copy-start.17 = (bf16[384,128]{1,0:T(8,128)(2,1)S(1)}, bf16[384,128]{1,0:T(8,128)(2,1)}, u32[]{:S(2)}) copy-start(bf16[384,128]{1,0:T(8,128)(2,1)} %param.35) | copy-start | bytes 294916
  1403.2 40.7 %reduce-scatter.24.cloned.1.call-start = ((), (), s32[]{:S(2)}) async-start(), calls=%async_computation.27 | async-start | bytes 491520 | tf_op jit(solution)/shard_map/reduce_scatter | solution.py:214
  1404.0 87.0 %reduce-scatter.36.cloned.1.call-start = ((), (), s32[]{:S(2)}) async-start(), calls=%async_computation.33 | async-start | bytes 589824 | tf_op jit(solution)/shard_map/reduce_scatter | solution.py:248
  1425.1 92.8 %reduce-scatter.38.cloned.1.call-start = ((), (), s32[]{:S(2)}) async-start(), calls=%async_computation.34 | async-start | bytes 589824 | tf_op jit(solution)/shard_map/reduce_scatter | solution.py:251
  1446.2 134.0 %reduce-scatter.34.cloned.1.call-start = ((), (), s32[]{:S(2)}) async-start(), calls=%async_computation.32 | async-start | bytes 6488064 | tf_op jit(solution)/shard_map/reduce_scatter | solution.py:266
  1460.5 182.4 %reduce-scatter.32.cloned.1.call-start = ((), (), s32[]{:S(2)}) async-start(), calls=%async_computation.31 | async-start | bytes 6488064 | tf_op jit(solution)/shard_map/reduce_scatter | solution.py:263
  1475.6 229.8 %reduce-scatter.30.cloned.1.call-start = ((), (), s32[]{:S(2)}) async-start(), calls=%async_computation.30 | async-start | bytes 6488064 | tf_op jit(solution)/shard_map/reduce_scatter | solution.py:260
  1490.9 27.0 %copy-start.12 = (bf16[3,512,512]{2,1,0:T(8,128)(2,1)S(1)}, bf16[3,512,512]{2,1,0:T(8,128)(2,1)}, u32[]{:S(2)}) copy-start(bf16[3,512,512]{2,1,0:T(8,128)(2,1)} %get-tuple-element.157) | copy-start | bytes 4718596
  1490.9 251.4 %all-reduce.7.cloned.1.call-start = ((), (), s32[]{:S(2)}) async-start(), calls=%async_computation.35 | async-start | bytes 262144 | tf_op jit(solution)/shard_map/psum | solution.py:226
  1517.8 268.7 %reduce-scatter.26.cloned.1.call-start = ((), (), s32[]{:S(2)}) async-start(), calls=%async_computation.28 | async-start | bytes 2359296 | tf_op jit(solution)/shard_map/reduce_scatter | solution.py:245
  1525.7 305.8 %reduce-scatter.28.cloned.1.call-start = ((), (), s32[]{:S(2)}) async-start(), calls=%async_computation.29 | async-start | bytes 2359296 | tf_op jit(solution)/shard_map/reduce_scatter | solution.py:254
  1533.7 410.9 %reduce-scatter.20.cloned.1.call-start = ((), (), s32[]{:S(2)}) async-start(), calls=%async_computation.25 | async-start | bytes 7864320 | tf_op jit(solution)/shard_map/reduce_scatter | solution.py:208
  1541.2 166.5 %copy-start.11 = (bf16[2048,128]{1,0:T(8,128)(2,1)S(1)}, bf16[2048,128]{1,0:T(8,128)(2,1)}, u32[]{:S(2)}) copy-start(bf16[2048,128]{1,0:T(8,128)(2,1)} %copy-done.10) | copy-start | bytes 1572868
  1541.2 166.5 %copy-start.19 = (bf16[384,128]{1,0:T(8,128)(2,1)S(1)}, bf16[384,128]{1,0:T(8,128)(2,1)}, u32[]{:S(2)}) copy-start(bf16[384,128]{1,0:T(8,128)(2,1)} %param.34) | copy-start | bytes 294916
  1541.3 166.5 %copy-start.20 = (bf16[384,128]{1,0:T(8,128)(2,1)S(1)}, bf16[384,128]{1,0:T(8,128)(2,1)}, u32[]{:S(2)}) copy-start(bf16[384,128]{1,0:T(8,128)(2,1)} %reduce-scatter.22.cloned.1.call-done) | copy-start | bytes 294916
  1645.2 299.4 %copy-start.1 = (bf16[384,2048]{1,0:T(8,128)(2,1)S(1)}, bf16[384,2048]{1,0:T(8,128)(2,1)}, u32[]{:S(2)}) copy-start(bf16[384,2048]{1,0:T(8,128)(2,1)} %param.20) | copy-start | bytes 4718596
  1645.2 299.4 %copy-start.9 = (bf16[2048,128]{1,0:T(8,128)(2,1)S(1)}, bf16[2048,128]{1,0:T(8,128)(2,1)}, u32[]{:S(2)}) copy-start(bf16[2048,128]{1,0:T(8,128)(2,1)} %copy-done.8) | copy-start | bytes 1572868
  1645.2 299.4 %copy-start.18 = (bf16[384,128]{1,0:T(8,128)(2,1)S(1)}, bf16[384,128]{1,0:T(8,128)(2,1)}, u32[]{:S(2)}) copy-start(bf16[384,128]{1,0:T(8,128)(2,1)} %reduce-scatter.24.cloned.1.call-done) | copy-start | bytes 294916
  1645.2 299.4 %copy-start.22 = (f32[8,1,256]{2,1,0:T(1,128)S(1)}, f32[8,1,256]{2,1,0:T(1,128)}, u32[]{:S(2)}) copy-start(f32[8,1,256]{2,1,0:T(1,128)} %copy-done.21) | copy-start | bytes 24580
  1645.3 299.4 %copy-start.26 = (f32[384]{0:T(512)S(1)}, f32[384]{0:T(512)}, u32[]{:S(2)}) copy-start(f32[384]{0:T(512)} %copy-done.25) | copy-start | bytes 4612
  1833.3 116.6 %copy-start.27 = (bf16[2048]{0:T(1024)(128)(2,1)S(1)}, bf16[2048]{0:T(1024)(128)(2,1)}, u32[]{:S(2)}) copy-start(bf16[2048]{0:T(1024)(128)(2,1)} %get-tuple-element.316) | copy-start | bytes 12292
  1833.3 143.0 %copy-start.28 = (f32[384]{0:T(512)S(1)}, f32[384]{0:T(512)}, u32[]{:S(2)}) copy-start(f32[384]{0:T(512)} %get-tuple-element.400) | copy-start | bytes 4612
  (16 other events, 36.2 us)
Sparse Core Ops, SparseCore 0:
  24.4 115.6 all-gather.11
  142.0 26.1 all-gather.13
  170.1 28.1 all-gather.15
  234.1 211.8 reduce-scatter.13
  447.8 44.3 all-gather.21
  494.1 115.3 all-gather.17
  611.4 41.5 all-gather.19
  654.6 115.3 all-gather.25
  771.8 42.5 all-gather.23
  870.6 211.8 reduce-scatter.17
  1084.8 111.7 reduce-scatter.15
  1203.4 115.8 all-gather.27
  1403.3 18.8 reduce-scatter.21
  1425.0 18.8 reduce-scatter.23
  1447.3 32.4 reduce-scatter.35
  1483.6 34.1 reduce-scatter.37
  1521.1 59.0 reduce-scatter.33
  1583.9 59.0 reduce-scatter.31
  1646.4 59.0 reduce-scatter.29
  1707.8 34.5 all-reduce.6
  1745.6 40.9 reduce-scatter.25
  1790.2 41.2 reduce-scatter.27
  1833.8 110.7 reduce-scatter.19
where the time goes:
time: 2000 us; the launch traced here: 1990 us
  waiting for transfers between devices  1530 us (76%)
  matrix products  286 us (14%)
  other arithmetic  72.1 us (4%)
  blocking collectives  63 us (3%)
  local copies, waits for them, and re-layouts  22.2 us (1%)
    reduce_scatter x1, waiting for transfers between devices, on_device(): lax.psum_scatter(jnp.dot(mixed, out_w, preferred_element_type=jnp.float32...  203 us
    reduce_scatter x1, waiting for transfers between devices, on_device(): lax.psum_scatter(contract_cols(gate_grad, gate_w) + contract_cols(up_grad...  197 us
    all_gather x1, waiting for transfers between devices, on_device(): ffn_normed = lax.all_gather(ffn_own, 'tensor', axis=0, tiled=True)  117 us
    all_gather x1, waiting for transfers between devices, on_device(): lax.all_gather(after_grad.astype(jnp.bfloat16), 'tensor', axis=0, tiled=T...  114 us
    reduce_scatter x1, waiting for transfers between devices, on_device(): lax.psum_scatter(normed_part.astype(jnp.bfloat16), 'tensor', scatter_dime...  111 us
    reduce_scatter x1, waiting for transfers between devices, on_device(): lax.psum_scatter(jnp.dot(hidden, down_w, preferred_element_type=jnp.float...  111 us
    all_gather x1, waiting for transfers between devices, on_device(): grad_full = lax.all_gather(d_out, 'tensor', axis=0, tiled=True)  102 us
    all_gather x1, waiting for transfers between devices, on_device(): normed = lax.all_gather(normed_own, 'tensor', axis=0, tiled=True)  95.1 us
  transfers between devices with their start and end apart: 23, of which 21 were waited for; matrix products, arithmetic and copies ran while one was open for 10% of the time, Pallas kernels for 0%

commit v1 on v0

--- a/solution.py
+++ b/solution.py
@@ -1,3 +1,4 @@
+import functools
 import jax
 import jax.numpy as jnp
 from jax import lax
@@ -6,6 +7,24 @@
 HD = 128
 QBLOCK = 512
 norm_eps = 1e-05
+
+
+def match_numbers(vec, group_axis):
+    then = lax.axis_index(group_axis)
+    y = lax.axis_size(group_axis)
+    arr_now, front, all_rows = (y, then, vec.shape[0])
+    made = [(dev, (dev + 1) % arr_now) for dev in range(arr_now)]
+    found_now = vec
+    t_next = jnp.zeros((*vec.shape[:0], arr_now * all_rows, *vec.shape[1:]), vec.dtype)
+    for u in range(arr_now):
+        y2 = (front - u) % arr_now
+        t_next = lax.dynamic_update_slice_in_dim(t_next, found_now, y2 * all_rows, axis=0)
+        if u < arr_now - 1:
+            found_now = lax.ppermute(found_now, axis_name=group_axis, perm=made)
+    return t_next
+
+
+_answer_waves = functools.partial(match_numbers, group_axis="tensor")
 
 
 def lookup(ids, table):
@@ -137,7 +156,7 @@
         tiled=True,
     ).astype(jnp.float32)
     output = (after_attn + ffn_part).astype(jnp.bfloat16)
-    grad_full = lax.all_gather(d_out, "tensor", axis=0, tiled=True)
+    grad_full = _answer_waves(d_out)
     down_grad = contract_rows(hidden, grad_full)
     hidden_grad = contract_cols(grad_full, down_w)
     gate_grad = (hidden_grad * upward * sigma * (1.0 + gate * (1.0 - sigma))).astype(jnp.bfloat16)

time: 2000 us -> 1930 us (0.965)
  waiting for transfers between devices: 1530 us -> 1430 us
  starting transfers between devices: 1.69 us -> 23.3 us
    ppermute x0 -> x3, waiting for transfers between devices: none -> 155 us  [match_numbers(): found_now = lax.ppermute(found_now, axis_name=group_axis, perm=made)]
    all_gather x1 -> x0, waiting for transfers between devices: 102 us -> none  [on_device(): grad_full = lax.all_gather(d_out, 'tensor', axis=0, tiled=True)]
    all_gather x1, waiting for transfers between devices: 117 us -> 22.4 us  [on_device(): ffn_normed = lax.all_gather(ffn_own, 'tensor', axis=0, tiled=True)]
    all_gather x1, waiting for transfers between devices: 39.5 us -> 0.01 us  [on_device(): lax.all_gather(w_up, 'dp', axis=0, tiled=True)]
    ppermute x0 -> x3, starting transfers between devices: none -> 21.7 us  [match_numbers(): found_now = lax.ppermute(found_now, axis_name=group_axis, perm=made)]
  transfers between devices with their start and end apart: 23 -> 25, of which waited for: 21 -> 22; matrix products, arithmetic and copies ran while one was open for 10% -> 11% of each run, Pallas kernels for 0% -> 0%
where the time goes in v1:
time: 1930 us
  waiting for transfers between devices  1430 us (74%)
  matrix products  286 us (15%)
  other arithmetic  72 us (4%)
  blocking collectives  63 us (3%)
  local copies, waits for them, and re-layouts  34.8 us (2%)
  starting transfers between devices  23.3 us (1%)
    reduce_scatter x1, waiting for transfers between devices, on_device(): lax.psum_scatter(jnp.dot(mixed, out_w, preferred_element_type=jnp.float32...  202 us
    reduce_scatter x1, waiting for transfers between devices, on_device(): lax.psum_scatter(contract_cols(gate_grad, gate_w) + contract_cols(up_grad...  197 us
    ppermute x3, waiting for transfers between devices, match_numbers(): found_now = lax.ppermute(found_now, axis_name=group_axis, perm=made)  155 us
    all_gather x1, waiting for transfers between devices, on_device(): lax.all_gather(after_grad.astype(jnp.bfloat16), 'tensor', axis=0, tiled=T...  114 us
    reduce_scatter x1, waiting for transfers between devices, on_device(): lax.psum_scatter(normed_part.astype(jnp.bfloat16), 'tensor', scatter_dime...  111 us
    reduce_scatter x1, waiting for transfers between devices, on_device(): lax.psum_scatter(jnp.dot(hidden, down_w, preferred_element_type=jnp.float...  111 us
    all_gather x1, waiting for transfers between devices, on_device(): normed = lax.all_gather(normed_own, 'tensor', axis=0, tiled=True)  95.1 us
    dot_general x7, matrix products, contract_cols(): lax.dot_general(left, right, (((1,), (1,)), ((), ())), preferred_element_...  77.6 us
  transfers between devices with their start and end apart: 25, of which 22 were waited for; matrix products, arithmetic and copies ran while one was open for 11% of the time, Pallas kernels for 0%

profile of v1, /device:TPU:0, one launch (start us, length us, event | category | flops | bytes accessed | tf_op | source)
XLA Modules:
  0.0 1927.7 jit_solution(1982337292291210324)
XLA Ops:
  10.4 10.3 all-gather
  26.3 9.8 all_gather.39
  36.1 8.9 all_gather.40
  45.0 95.1 %all-gather.11.cloned.1.call-done = bf16[1536,2048]{1,0:T(8,128)(2,1)} async-done(((bf16[384,2048]{1,0:T(8,128)(2,1)}), bf16[1536,2048]{1,0:T(8,128)(2,1)}) %all-gather.11.cloned.1.call-update) | async-done | bytes 6291472 | tf_op jit(solution)/shard_map/all_gather | solution.py:100
  144.9 23.3 %all-gather.13.cloned.1.call-done = bf16[2048,512]{1,0:T(8,128)(2,1)} async-done(((bf16[256,512]{1,0:T(8,128)(2,1)}), bf16[2048,512]{1,0:T(8,128)(2,1)}) %all-gather.13.cloned.1.call-update) | async-done | bytes 2097168 | tf_op jit(solution)/shard_map/all_gather | solution.py:84
  168.2 8.0 convolution_convert_fusion.8
  184.9 40.4 %while.27 = (s32[]{:T(128)}, bf16[3,512,512]{2,1,0:T(8,128)(2,1)S(1)}, f32[3,4,512]{2,1,0:T(4,128)S(1)}, s32[1536]{0:T(1024)S(1)}, s32[3,512]{1,0:T(4,128)S(1)},...) while((s32[]{:T(128)}, ...), condition=%wide.region_6.7_spmd, body=%wide.region_3.6_spmd.sunk | while | flops 1654126592 | bytes 44929176 | solution.py:136
  225.4 8.6 fusion.48
  234.7 8.8 all-gather.1
  243.5 202.5 %reduce-scatter.14.cloned.1.call-done = f32[384,2048]{1,0:T(8,128)} async-done(((f32[1536,2048]{1,0:T(8,128)}), f32[384,2048]{1,0:T(8,128)}) %reduce-scatter.14.cloned.1.call-update) | async-done | bytes 3145744 | tf_op jit(solution)/shard_map/reduce_scatter | solution.py:138
  453.4 36.7 %collective-permute-done = bf16[384,2048]{1,0:T(8,128)(2,1)S(1)} collective-permute-done((bf16[384,2048]{1,0:T(8,128)(2,1)}, bf16[384,2048]{1,0:T(8,128)(2,1)S(1)}, u32[]{:S(2)}, u32[]{:S(2)}) %collective-permute-start) | collective-permute-done | bytes 1572896 | tf_op jit(solution)/shard_map/ppermute | solution.py:23
  491.3 60.1 %collective-permute-done.1 = bf16[384,2048]{1,0:T(8,128)(2,1)} collective-permute-done((bf16[384,2048]{1,0:T(8,128)(2,1)S(1)}, bf16[384,2048]{1,0:T(8,128)(2,1)}, u32[]{:S(2)}, u32[]{:S(2)}) %collective-permute-start.1) | collective-permute-done | bytes 1572896 | tf_op jit(solution)/shard_map/ppermute | solution.py:23
  551.4 20.1 %collective-permute-start.2 = (bf16[384,2048]{1,0:T(8,128)(2,1)}, bf16[384,2048]{1,0:T(8,128)(2,1)}, u32[]{:S(2)}, u32[]{:S(2)}) collective-permute-start(bf16[384,2048]{1,0:T(8,128)(2,1)} %collective-permute-done.1), channel_id=1, source_target_pairs={{0,1},{1,2},{2,3},{3,0},{4,5},{5,6},{6,7},{7,4},{8,9},{9,10},{10,1... | collective-permute-start | bytes 4718600 | tf_op jit(solution)/shard_map/ppermute | solution.py:23
  580.2 58.4 %collective-permute-done.2 = bf16[384,2048]{1,0:T(8,128)(2,1)} collective-permute-done((bf16[384,2048]{1,0:T(8,128)(2,1)}, bf16[384,2048]{1,0:T(8,128)(2,1)}, u32[]{:S(2)}, u32[]{:S(2)}) %collective-permute-start.2) | collective-permute-done | bytes 1572896 | tf_op jit(solution)/shard_map/ppermute | solution.py:23
  641.4 22.4 %all-gather.17.cloned.1.call-done = bf16[1536,2048]{1,0:T(8,128)(2,1)} async-done(((bf16[384,2048]{1,0:T(8,128)(2,1)}), bf16[1536,2048]{1,0:T(8,128)(2,1)}) %all-gather.17.cloned.1.call-update) | async-done | bytes 6291472 | tf_op jit(solution)/shard_map/all_gather | solution.py:147
  663.7 15.3 fusion.50
  679.0 28.2 %all-gather.19.cloned.1.call-done = bf16[2048,1408]{1,0:T(8,128)(2,1)} async-done(((bf16[256,1408]{1,0:T(8,128)(2,1)}), bf16[2048,1408]{1,0:T(8,128)(2,1)}) %all-gather.19.cloned.1.call-update) | async-done | bytes 5767184 | tf_op jit(solution)/shard_map/all_gather | solution.py:91
  707.2 15.1 fusion.49
  722.4 31.1 %all-gather.23.cloned.1.call-done = bf16[1408,2048]{1,0:T(8,128)(2,1)} async-done(((bf16[1408,256]{1,0:T(8,128)(2,1)}), bf16[1408,2048]{1,0:T(8,128)(2,1)}) %all-gather.23.cloned.1.call-update) | async-done | bytes 5767184 | tf_op jit(solution)/shard_map/all_gather | solution.py:93
  753.5 22.9 %multiply_convert_fusion = (bf16[1536,1408]{1,0:T(8,128)(2,1)}, bf16[1536,1408]{1,0:T(8,128)(2,1)}, bf16[1536,1408]{1,0:T(8,128)(2,1)}) fusion(f32[1536,1408]{1,0:T(8,128)} %fusion.49, f32[1536,1408]{1,0:T(8,128)} %fusion.50, bf16[1536,2048]{1,0:T(8,128)(2,1)} %constant_dynamic-update-slice_fusion.2, bf16[1408,2048]{1,0:T(8,128)(2,1)} %all-gather.23.cloned.1.call-done), kind=kOutput, calls=%fused_computation.58 | convolution fusion | flops 8892973056 | bytes 42336256 | tf_op jit(solution)/shard_map/dot_general | solution.py:58
  776.4 16.6 fusion.51
  793.1 16.4 convolution_add_fusion
  809.6 15.0 convolution_convert_fusion.4
  824.7 196.9 %reduce-scatter.18.cloned.1.call-done = f32[384,2048]{1,0:T(8,128)} async-done(((f32[1536,2048]{1,0:T(8,128)}), f32[384,2048]{1,0:T(8,128)}) %reduce-scatter.18.cloned.1.call-update) | async-done | bytes 3145744 | tf_op jit(solution)/shard_map/reduce_scatter | solution.py:166
  1024.8 110.7 %reduce-scatter.16.cloned.1.call-done = bf16[384,2048]{1,0:T(8,128)(2,1)} async-done(((bf16[1536,2048]{1,0:T(8,128)(2,1)}), bf16[384,2048]{1,0:T(8,128)(2,1)}) %reduce-scatter.16.cloned.1.call-update) | async-done | bytes 1572880 | tf_op jit(solution)/shard_map/reduce_scatter | solution.py:152
  1135.5 6.7 fusion.47
  1144.2 114.0 %all-gather.25.cloned.1.call-done = bf16[1536,2048]{1,0:T(8,128)(2,1)} async-done(((bf16[384,2048]{1,0:T(8,128)(2,1)}), bf16[1536,2048]{1,0:T(8,128)(2,1)}) %all-gather.25.cloned.1.call-update) | async-done | bytes 6291472 | tf_op jit(solution)/shard_map/all_gather | solution.py:176
  1258.2 6.9 convolution_convert_fusion.7
  1268.4 71.4 %while.28 = (s32[]{:T(128)}, f32[1536,128]{1,0:T(8,128)}, f32[1536,128]{1,0:T(8,128)S(1)}, bf16[3,512,512]{2,1,0:T(8,128)(2,1)}, s32[1536]{0:T(1024)S(1)}, /*ind...) while((s32[]{:T(128)}, f32[1536,128]{1,0:T(8,128)}, ...), condition=%wide.region_14.15_spmd.clone, body=%wide.region_12.14_spmd.clone.sunk | while | flops 4061853696 | bytes 139145552 | solution.py:220
  1273.7 5.6 fusion.117
  1343.0 17.8 reduce-scatter.22.cloned.1.call-done
  1363.8 18.9 reduce-scatter.24.cloned.1.call-done
  1385.1 14.3 convolution_convert_fusion
  1399.4 15.0 convolution_convert_fusion.1
  1414.8 15.0 convolution_convert_fusion.2
  1429.9 26.8 %reduce-scatter.38.cloned.1.call-done = bf16[256,128]{1,0:T(8,128)(2,1)} async-done(((bf16[2048,128]{1,0:T(8,128)(2,1)}), bf16[256,128]{1,0:T(8,128)(2,1)}) %reduce-scatter.38.cloned.1.call-update) | async-done | bytes 65552 | tf_op jit(solution)/shard_map/reduce_scatter | solution.py:270
  1456.7 7.8 convolution_convert_fusion.6
  1464.6 7.9 convolution_convert_fusion.5
  1472.9 7.2 convolution_convert_fusion.3
  1481.9 37.1 %reduce-scatter.34.cloned.1.call-done = bf16[1408,256]{1,0:T(8,128)(2,1)} async-done(((bf16[1408,2048]{1,0:T(8,128)(2,1)}), bf16[1408,256]{1,0:T(8,128)(2,1)}) %reduce-scatter.34.cloned.1.call-update) | async-done | bytes 720912 | tf_op jit(solution)/shard_map/reduce_scatter | solution.py:285
  1521.4 60.4 %reduce-scatter.32.cloned.1.call-done = bf16[256,1408]{1,0:T(8,128)(2,1)} async-done(((bf16[2048,1408]{1,0:T(8,128)(2,1)}), bf16[256,1408]{1,0:T(8,128)(2,1)}) %reduce-scatter.32.cloned.1.call-update) | async-done | bytes 720912 | tf_op jit(solution)/shard_map/reduce_scatter | solution.py:282
  1584.1 60.1 %reduce-scatter.30.cloned.1.call-done = bf16[256,1408]{1,0:T(8,128)(2,1)} async-done(((bf16[2048,1408]{1,0:T(8,128)(2,1)}), bf16[256,1408]{1,0:T(8,128)(2,1)}) %reduce-scatter.30.cloned.1.call-update) | async-done | bytes 720912 | tf_op jit(solution)/shard_map/reduce_scatter | solution.py:279
  1648.8 32.5 %all-reduce.7.cloned.1.call-done = (bf16[256,128]{1,0:T(8,128)(2,1)}, bf16[256,128]{1,0:T(8,128)(2,1)}) async-done(((bf16[256,128]{1,0:T(8,128)(2,1)}, bf16[256,128]{1,0:T(8,128)(2,1)}), (bf16[256,128]{1,0:T(8,128)(2,1)}, bf16[256,128]{1,0:T(8,128)(2,1)})) %all-reduce.7.cloned.1.call-update) | async-done | bytes 131088 | tf_op jit(solution)/shard_map/psum | solution.py:245
  1684.3 41.1 %reduce-scatter.26.cloned.1.call-done = bf16[256,512]{1,0:T(8,128)(2,1)} async-done(((bf16[2048,512]{1,0:T(8,128)(2,1)}), bf16[256,512]{1,0:T(8,128)(2,1)}) %reduce-scatter.26.cloned.1.call-update) | async-done | bytes 262160 | tf_op jit(solution)/shard_map/reduce_scatter | solution.py:264
  1727.2 43.1 %reduce-scatter.28.cloned.1.call-done = bf16[512,256]{1,0:T(8,128)(2,1)} async-done(((bf16[512,2048]{1,0:T(8,128)(2,1)}), bf16[512,256]{1,0:T(8,128)(2,1)}) %reduce-scatter.28.cloned.1.call-update) | async-done | bytes 262160 | tf_op jit(solution)/shard_map/reduce_scatter | solution.py:273
  1772.1 111.3 %reduce-scatter.20.cloned.1.call-done = bf16[384,2048]{1,0:T(8,128)(2,1)} async-done(((bf16[1536,2048]{1,0:T(8,128)(2,1)}), bf16[384,2048]{1,0:T(8,128)(2,1)}) %reduce-scatter.20.cloned.1.call-update) | async-done | bytes 1572880 | tf_op jit(solution)/shard_map/reduce_scatter | solution.py:227
  1888.7 14.0 all-reduce.2
  1902.8 11.1 all-reduce.3
  (257 shorter events, 195.5 us)
Async XLA Ops:
  7.2 18.7 copy-start.18
  7.2 18.7 copy-start.32
  7.2 19.1 copy-start.19
  7.2 19.1 copy-start.26
  7.2 28.9 %copy-start.27 = (bf16[256,128]{1,0:T(8,128)(2,1)S(1)}, bf16[256,128]{1,0:T(8,128)(2,1)}, u32[]{:S(2)}) copy-start(bf16[256,128]{1,0:T(8,128)(2,1)} %param.24) | copy-start | bytes 196612
  7.2 132.9 %all-gather.11.cloned.1.call-start = ((), (), s32[]{:S(2)}) async-start(), calls=%async_computation.13 | async-start | bytes 7864320 | tf_op jit(solution)/shard_map/all_gather | solution.py:100
  10.4 134.3 %copy-start.28 = (f32[384]{0:T(512)}, f32[384]{0:T(512)S(1)}, u32[]{:S(2)}) copy-start(f32[384]{0:T(512)S(1)} %get-tuple-element.401) | copy-start | bytes 4612
  24.3 143.9 %all-gather.13.cloned.1.call-start = ((), (), s32[]{:S(2)}) async-start(), calls=%async_computation.14 | async-start | bytes 2359296 | tf_op jit(solution)/shard_map/all_gather | solution.py:84
  25.1 200.3 %all-gather.15.cloned.1.call-start = ((), (), s32[]{:S(2)}) async-start(), calls=%async_computation.15 | async-start | bytes 2359296 | tf_op jit(solution)/shard_map/all_gather | solution.py:87
  25.8 420.2 %reduce-scatter.14.cloned.1.call-start = ((), (), s32[]{:S(2)}) async-start(), calls=%async_computation.16 | async-start | bytes 15728640 | tf_op jit(solution)/shard_map/reduce_scatter | solution.py:138
  36.1 144.1 %copy-start.11 = (bf16[2048,128]{1,0:T(8,128)(2,1)}, bf16[2048,128]{1,0:T(8,128)(2,1)S(1)}, u32[]{:S(2)}) copy-start(bf16[2048,128]{1,0:T(8,128)(2,1)S(1)} %all_gather.39) | copy-start | bytes 1572868
  45.0 123.2 %copy-start.9 = (bf16[2048,128]{1,0:T(8,128)(2,1)}, bf16[2048,128]{1,0:T(8,128)(2,1)S(1)}, u32[]{:S(2)}) copy-start(bf16[2048,128]{1,0:T(8,128)(2,1)S(1)} %all_gather.40) | copy-start | bytes 1572868
  144.7 31.4 %copy-start.5 = (bf16[1536,128]{1,0:T(8,128)(2,1)}, bf16[1536,128]{1,0:T(8,128)(2,1)S(1)}, u32[]{:S(2)}) copy-start(bf16[1536,128]{1,0:T(8,128)(2,1)S(1)} %convolution_convert_fusion.11) | copy-start | bytes 1179652
  234.0 407.4 %all-gather.21.cloned.1.call-start = ((), (), s32[]{:S(2)}) async-start(), calls=%async_computation.19 | async-start | bytes 6488064 | tf_op jit(solution)/shard_map/all_gather | solution.py:92
  234.6 429.1 %all-gather.17.cloned.1.call-start = ((), (), s32[]{:S(2)}) async-start(), calls=%async_computation.17 | async-start | bytes 7864320 | tf_op jit(solution)/shard_map/all_gather | solution.py:147
  450.4 256.9 %all-gather.19.cloned.1.call-start = ((), (), s32[]{:S(2)}) async-start(), calls=%async_computation.18 | async-start | bytes 6488064 | tf_op jit(solution)/shard_map/all_gather | solution.py:91
  451.1 302.4 %all-gather.23.cloned.1.call-start = ((), (), s32[]{:S(2)}) async-start(), calls=%async_computation.20 | async-start | bytes 6488064 | tf_op jit(solution)/shard_map/all_gather | solution.py:93
  451.9 569.7 %reduce-scatter.18.cloned.1.call-start = ((), (), s32[]{:S(2)}) async-start(), calls=%async_computation.22 | async-start | bytes 15728640 | tf_op jit(solution)/shard_map/reduce_scatter | solution.py:166
  451.9 38.2 %collective-permute-start = (bf16[384,2048]{1,0:T(8,128)(2,1)}, bf16[384,2048]{1,0:T(8,128)(2,1)S(1)}, u32[]{:S(2)}, u32[]{:S(2)}) collective-permute-start(bf16[384,2048]{1,0:T(8,128)(2,1)} %param.33), channel_id=1, source_target_pairs={{0,1},{1,2},{2,3},{3,0},{4,5},{5,6},{6,7},{7,4},{8,9},{9,10},{10,1... | collective-permute-start | bytes 4718600 | tf_op jit(solution)/shard_map/ppermute | solution.py:23
  491.3 60.1 %collective-permute-start.1 = (bf16[384,2048]{1,0:T(8,128)(2,1)S(1)}, bf16[384,2048]{1,0:T(8,128)(2,1)}, u32[]{:S(2)}, u32[]{:S(2)}) collective-permute-start(bf16[384,2048]{1,0:T(8,128)(2,1)S(1)} %collective-permute-done), channel_id=1, source_target_pairs={{0,1},{1,2},{2,3},{3,0},{4,5},{5,6},{6,7},{7,4},{8,9},{9,10},{10,1... | collective-permute-start | bytes 4718600 | tf_op jit(solution)/shard_map/ppermute | solution.py:23
  551.4 87.3 %collective-permute-start.2 = (bf16[384,2048]{1,0:T(8,128)(2,1)}, bf16[384,2048]{1,0:T(8,128)(2,1)}, u32[]{:S(2)}, u32[]{:S(2)}) collective-permute-start(bf16[384,2048]{1,0:T(8,128)(2,1)} %collective-permute-done.1), channel_id=1, source_target_pairs={{0,1},{1,2},{2,3},{3,0},{4,5},{5,6},{6,7},{7,4},{8,9},{9,10},{10,1... | collective-permute-start | bytes 4718600 | tf_op jit(solution)/shard_map/ppermute | solution.py:23
  776.4 16.6 copy-start.35
  809.5 326.0 %reduce-scatter.16.cloned.1.call-start = ((), (), s32[]{:S(2)}) async-start(), calls=%async_computation.21 | async-start | bytes 7864320 | tf_op jit(solution)/shard_map/reduce_scatter | solution.py:152
  824.6 433.6 %all-gather.25.cloned.1.call-start = ((), (), s32[]{:S(2)}) async-start(), calls=%async_computation.23 | async-start | bytes 7864320 | tf_op jit(solution)/shard_map/all_gather | solution.py:176
  1142.2 218.7 %reduce-scatter.22.cloned.1.call-start = ((), (), s32[]{:S(2)}) async-start(), calls=%async_computation.25 | async-start | bytes 491520 | tf_op jit(solution)/shard_map/reduce_scatter | solution.py:230
  1339.8 42.9 %copy-start.4 = (bf16[384,2048]{1,0:T(8,128)(2,1)S(1)}, bf16[384,2048]{1,0:T(8,128)(2,1)}, u32[]{:S(2)}) copy-start(bf16[384,2048]{1,0:T(8,128)(2,1)} %fusion.39) | copy-start | bytes 4718596
  1339.8 42.9 %copy-start.20 = (bf16[384,128]{1,0:T(8,128)(2,1)S(1)}, bf16[384,128]{1,0:T(8,128)(2,1)}, u32[]{:S(2)}) copy-start(bf16[384,128]{1,0:T(8,128)(2,1)} %param.35) | copy-start | bytes 294916
  1341.9 40.8 %reduce-scatter.24.cloned.1.call-start = ((), (), s32[]{:S(2)}) async-start(), calls=%async_computation.26 | async-start | bytes 491520 | tf_op jit(solution)/shard_map/reduce_scatter | solution.py:233
  1342.8 87.1 %reduce-scatter.36.cloned.1.call-start = ((), (), s32[]{:S(2)}) async-start(), calls=%async_computation.32 | async-start | bytes 589824 | tf_op jit(solution)/shard_map/reduce_scatter | solution.py:267
  1363.8 92.9 %reduce-scatter.38.cloned.1.call-start = ((), (), s32[]{:S(2)}) async-start(), calls=%async_computation.33 | async-start | bytes 589824 | tf_op jit(solution)/shard_map/reduce_scatter | solution.py:270
  1385.0 134.0 %reduce-scatter.34.cloned.1.call-start = ((), (), s32[]{:S(2)}) async-start(), calls=%async_computation.31 | async-start | bytes 6488064 | tf_op jit(solution)/shard_map/reduce_scatter | solution.py:285
  1399.4 182.4 %reduce-scatter.32.cloned.1.call-start = ((), (), s32[]{:S(2)}) async-start(), calls=%async_computation.30 | async-start | bytes 6488064 | tf_op jit(solution)/shard_map/reduce_scatter | solution.py:282
  1414.5 229.7 %reduce-scatter.30.cloned.1.call-start = ((), (), s32[]{:S(2)}) async-start(), calls=%async_computation.29 | async-start | bytes 6488064 | tf_op jit(solution)/shard_map/reduce_scatter | solution.py:279
  1429.8 26.9 %copy-start.13 = (bf16[3,512,512]{2,1,0:T(8,128)(2,1)S(1)}, bf16[3,512,512]{2,1,0:T(8,128)(2,1)}, u32[]{:S(2)}) copy-start(bf16[3,512,512]{2,1,0:T(8,128)(2,1)} %get-tuple-element.157) | copy-start | bytes 4718596
  1429.8 251.5 %all-reduce.7.cloned.1.call-start = ((), (), s32[]{:S(2)}) async-start(), calls=%async_computation.34 | async-start | bytes 262144 | tf_op jit(solution)/shard_map/psum | solution.py:245
  1456.7 268.7 %reduce-scatter.26.cloned.1.call-start = ((), (), s32[]{:S(2)}) async-start(), calls=%async_computation.27 | async-start | bytes 2359296 | tf_op jit(solution)/shard_map/reduce_scatter | solution.py:264
  1464.5 305.8 %reduce-scatter.28.cloned.1.call-start = ((), (), s32[]{:S(2)}) async-start(), calls=%async_computation.28 | async-start | bytes 2359296 | tf_op jit(solution)/shard_map/reduce_scatter | solution.py:273
  1472.5 410.8 %reduce-scatter.20.cloned.1.call-start = ((), (), s32[]{:S(2)}) async-start(), calls=%async_computation.24 | async-start | bytes 7864320 | tf_op jit(solution)/shard_map/reduce_scatter | solution.py:227
  1480.0 166.4 %copy-start.12 = (bf16[2048,128]{1,0:T(8,128)(2,1)S(1)}, bf16[2048,128]{1,0:T(8,128)(2,1)}, u32[]{:S(2)}) copy-start(bf16[2048,128]{1,0:T(8,128)(2,1)} %copy-done.11) | copy-start | bytes 1572868
  1480.1 166.4 %copy-start.22 = (bf16[384,128]{1,0:T(8,128)(2,1)S(1)}, bf16[384,128]{1,0:T(8,128)(2,1)}, u32[]{:S(2)}) copy-start(bf16[384,128]{1,0:T(8,128)(2,1)} %param.34) | copy-start | bytes 294916
  1480.1 166.4 %copy-start.23 = (bf16[384,128]{1,0:T(8,128)(2,1)S(1)}, bf16[384,128]{1,0:T(8,128)(2,1)}, u32[]{:S(2)}) copy-start(bf16[384,128]{1,0:T(8,128)(2,1)} %reduce-scatter.22.cloned.1.call-done) | copy-start | bytes 294916
  1584.1 299.3 %copy-start.1 = (bf16[384,2048]{1,0:T(8,128)(2,1)S(1)}, bf16[384,2048]{1,0:T(8,128)(2,1)}, u32[]{:S(2)}) copy-start(bf16[384,2048]{1,0:T(8,128)(2,1)} %param.20) | copy-start | bytes 4718596
  1584.1 299.3 %copy-start.10 = (bf16[2048,128]{1,0:T(8,128)(2,1)S(1)}, bf16[2048,128]{1,0:T(8,128)(2,1)}, u32[]{:S(2)}) copy-start(bf16[2048,128]{1,0:T(8,128)(2,1)} %copy-done.9) | copy-start | bytes 1572868
  1584.1 299.3 %copy-start.21 = (bf16[384,128]{1,0:T(8,128)(2,1)S(1)}, bf16[384,128]{1,0:T(8,128)(2,1)}, u32[]{:S(2)}) copy-start(bf16[384,128]{1,0:T(8,128)(2,1)} %reduce-scatter.24.cloned.1.call-done) | copy-start | bytes 294916
  1584.1 299.3 %copy-start.25 = (f32[8,1,256]{2,1,0:T(1,128)S(1)}, f32[8,1,256]{2,1,0:T(1,128)}, u32[]{:S(2)}) copy-start(f32[8,1,256]{2,1,0:T(1,128)} %copy-done.24) | copy-start | bytes 24580
  1584.1 299.3 %copy-start.29 = (f32[384]{0:T(512)S(1)}, f32[384]{0:T(512)}, u32[]{:S(2)}) copy-start(f32[384]{0:T(512)} %copy-done.28) | copy-start | bytes 4612
  1772.1 116.6 %copy-start.30 = (bf16[2048]{0:T(1024)(128)(2,1)S(1)}, bf16[2048]{0:T(1024)(128)(2,1)}, u32[]{:S(2)}) copy-start(bf16[2048]{0:T(1024)(128)(2,1)} %get-tuple-element.316) | copy-start | bytes 12292
  1772.1 143.0 %copy-start.31 = (f32[384]{0:T(512)S(1)}, f32[384]{0:T(512)}, u32[]{:S(2)}) copy-start(f32[384]{0:T(512)} %get-tuple-element.400) | copy-start | bytes 4612
  (21 other events, 62.8 us)
Sparse Core Ops, SparseCore 0:
  24.4 115.6 all-gather.10
  142.0 26.1 all-gather.12
  170.0 28.1 all-gather.14
  234.1 211.8 reduce-scatter.13
  447.7 44.3 all-gather.20
  494.1 169.5 all-gather.16
  665.6 41.5 all-gather.18
  709.1 44.3 all-gather.22
  809.6 211.8 reduce-scatter.17
  1023.7 111.7 reduce-scatter.15
  1142.3 115.8 all-gather.24
  1342.0 18.7 reduce-scatter.21
  1363.8 18.8 reduce-scatter.23
  1386.2 32.3 reduce-scatter.35
  1422.4 34.1 reduce-scatter.37
  1459.9 59.0 reduce-scatter.33
  1522.7 59.0 reduce-scatter.31
  1585.1 59.0 reduce-scatter.29
  1646.7 34.5 all-reduce.6
  1684.4 40.9 reduce-scatter.25
  1729.0 41.2 reduce-scatter.27
  1772.6 110.7 reduce-scatter.19
